TPU v7x, 32 devices: a whole 2x2x4 slice. The times are simulated.
32 devices in a mesh: dp: 16 (over z, y, x), tensor: 2 (over core).
Axes of the slice: x: 2, y: 2, z: 4, core: 2. Of those that a mesh axis runs over, the one named last changes fastest.
Arguments:
- text_input: bfloat16 [32, 512, 768], P(('dp', 'tensor')), may hold values from -6 to 6
- layout_input: bfloat16 [32, 512, 192], P(('dp', 'tensor')), may hold values from -6 to 6
- page_counts: int32 [32], P(('dp', 'tensor')), may hold values from 16 to 512, as said below
- text_joint: bfloat16 [768, 2304], replicated, may hold values from -0.21875 to 0.21875
- text_mixing: bfloat16 [768, 768], replicated, may hold values from -0.625 to 0.625
- text_norms: float32 [4, 768], replicated, may hold values from 0.1 to 1.9
- text_upward: bfloat16 [768, 3072], P(None, 'tensor'), may hold values from -0.21875 to 0.21875
- text_downward: bfloat16 [3072, 768], P('tensor'), may hold values from -0.109375 to 0.109375
- layout_joint: bfloat16 [192, 576], replicated, may hold values from -0.4375 to 0.4375
- layout_mixing: bfloat16 [192, 192], replicated, may hold values from -1.25 to 1.25
- layout_norms: float32 [4, 192], replicated, may hold values from 0.1 to 1.9
- layout_upward: bfloat16 [192, 768], P(None, 'tensor'), may hold values from -0.4375 to 0.4375
- layout_downward: bfloat16 [768, 192], P('tensor'), may hold values from -0.21875 to 0.21875
- text_cotangent: bfloat16 [32, 512, 768], P(('dp', 'tensor')), may hold values from -6 to 6
- layout_cotangent: bfloat16 [32, 512, 192], P(('dp', 'tensor')), may hold values from -6 to 6
Outputs:
- text_result: bfloat16 [32, 512, 768], P(('dp', 'tensor'))
- layout_result: bfloat16 [32, 512, 192], P(('dp', 'tensor'))
- text_gradient: float32 [32, 512, 768], P(('dp', 'tensor'))
- layout_gradient: float32 [32, 512, 192], P(('dp', 'tensor'))
- joint_text_gradient: float32 [768, 2304], replicated
- mixing_text_gradient: float32 [768, 768], replicated
- norms_text_gradient: float32 [4, 768], replicated
- upward_text_gradient: float32 [768, 3072], P(None, 'tensor')
- downward_text_gradient: float32 [3072, 768], P('tensor')
- joint_layout_gradient: float32 [192, 576], replicated
- mixing_layout_gradient: float32 [192, 192], replicated
- norms_layout_gradient: float32 [4, 192], replicated
- upward_layout_gradient: float32 [192, 768], P(None, 'tensor')
- downward_layout_gradient: float32 [768, 192], P('tensor')
Inputs may be any that keep to these rules, and one draw needn't show every extreme that they name: `page_counts`: keys of a page in slots below its count are live; some page has all 512 slots live; counts are spread over several powers of two.
All inputs are finite; a program needn't handle non-finite values.
Results may differ from a plain program's by a relative error of at most 0.015.
Values may be sent and summed in bfloat16 or wider, within the bound.
No kernel may reach another device: no remote copies, remote signals or barrier semaphores. Data moves between devices by JAX's collectives and lax.ppermute only.
A program may use at most 192 MiB of HBM per device.

v0:
```python
import math
import jax
import jax.numpy as jnp
from jax import lax
from jax.sharding import PartitionSpec as P

HEADS = 12
NEG_FILL = -1e30


def normalize(hidden, gain, shift):
    center = hidden - jnp.mean(hidden, axis=-1, keepdims=True)
    spread = jnp.mean(center * center, axis=-1, keepdims=True)
    return center * lax.rsqrt(spread + 1e-05) * gain + shift


def gelu_exact(value):
    return jax.nn.gelu(value, approximate=False)


def scores_of(queries, keys_in, scale):
    return jnp.einsum("qhd,khd->hqk", queries, keys_in, preferred_element_type=jnp.float32) * scale


def logits_pair(text_grid, layout_grid, count):
    slots = text_grid.shape[0]
    text_score = scores_of(text_grid[:, 0], text_grid[:, 1], 1.0 / math.sqrt(text_grid.shape[-1]))
    layout_score = scores_of(
        layout_grid[:, 0], layout_grid[:, 1], 1.0 / math.sqrt(layout_grid.shape[-1])
    )
    live = (jnp.arange(slots) < count)[None, None, :]
    return (
        jnp.where(live, text_score + layout_score, NEG_FILL),
        jnp.where(live, layout_score + text_score, NEG_FILL),
    )


def attend(logits, values):
    top = jnp.max(logits, axis=-1, keepdims=True)
    total = top + jnp.log(jnp.sum(jnp.exp(logits - top), axis=-1, keepdims=True))
    weights = jnp.exp(logits - total).astype(jnp.bfloat16)
    mixed = jnp.einsum("hqk,khd->qhd", weights, values, preferred_element_type=jnp.float32)
    return (mixed.astype(jnp.bfloat16), total)


def page_forward(items):
    text_grid, layout_grid, count = items
    text_logits, layout_logits = logits_pair(text_grid, layout_grid, count)
    text_mixed, text_total = attend(text_logits, text_grid[:, 2])
    layout_mixed, layout_total = attend(layout_logits, layout_grid[:, 2])
    return (text_mixed, layout_mixed, text_total, layout_total)


def probs_back(logits, total, values, upstream):
    probs = jnp.exp(logits - total)
    value_grad = jnp.einsum(
        "hqk,qhd->khd", probs.astype(jnp.bfloat16), upstream, preferred_element_type=jnp.float32
    )
    prob_grad = jnp.einsum("qhd,khd->hqk", upstream, values, preferred_element_type=jnp.float32)
    logit_grad = probs * (prob_grad - jnp.sum(prob_grad * probs, axis=-1, keepdims=True))
    return (logit_grad, value_grad)


def joint_grads(grid, score_grad, value_grad):
    scale = 1.0 / math.sqrt(grid.shape[-1])
    query_grad = (
        jnp.einsum("hqk,khd->qhd", score_grad, grid[:, 1], preferred_element_type=jnp.float32)
        * scale
    )
    key_grad = (
        jnp.einsum("hqk,qhd->khd", score_grad, grid[:, 0], preferred_element_type=jnp.float32)
        * scale
    )
    return jnp.stack([query_grad, key_grad, value_grad], axis=1).astype(jnp.bfloat16)


def page_backward(items):
    text_grid, layout_grid, count, text_total, layout_total, text_upper, layout_upper = items
    text_logits, layout_logits = logits_pair(text_grid, layout_grid, count)
    text_lgrad, text_vgrad = probs_back(text_logits, text_total, text_grid[:, 2], text_upper)
    layout_lgrad, layout_vgrad = probs_back(
        layout_logits, layout_total, layout_grid[:, 2], layout_upper
    )
    text_sgrad = text_lgrad.astype(jnp.bfloat16)
    layout_sgrad = (text_lgrad + layout_lgrad).astype(jnp.bfloat16)
    return (
        joint_grads(text_grid, text_sgrad, text_vgrad),
        joint_grads(layout_grid, layout_sgrad, layout_vgrad),
    )


def matmul(left, right):
    return jnp.dot(left, right, preferred_element_type=jnp.float32)


def shards(
    text_input,
    layout_input,
    page_counts,
    text_joint,
    text_mixing,
    text_norms,
    text_upward,
    text_downward,
    layout_joint,
    layout_mixing,
    layout_norms,
    layout_upward,
    layout_downward,
    text_cotangent,
    layout_cotangent,
):
    pages, slots, width_text = text_input.shape
    width_layout = layout_input.shape[2]
    text_rows = text_input.reshape(-1, width_text)
    layout_rows = layout_input.reshape(-1, width_layout)
    text_grid = (
        matmul(text_rows, text_joint).astype(jnp.bfloat16).reshape(pages, slots, 3, HEADS, -1)
    )
    layout_grid = (
        matmul(layout_rows, layout_joint).astype(jnp.bfloat16).reshape(pages, slots, 3, HEADS, -1)
    )
    text_mixed, layout_mixed, text_total, layout_total = lax.map(
        page_forward, (text_grid, layout_grid, page_counts)
    )
    text_mixed = text_mixed.reshape(-1, width_text)
    layout_mixed = layout_mixed.reshape(-1, width_layout)
    text_resid = text_rows.astype(jnp.float32) + matmul(text_mixed, text_mixing)
    layout_resid = layout_rows.astype(jnp.float32) + matmul(layout_mixed, layout_mixing)
    text_first, text_pull_one = jax.vjp(normalize, text_resid, text_norms[0], text_norms[1])
    layout_first, layout_pull_one = jax.vjp(
        normalize, layout_resid, layout_norms[0], layout_norms[1]
    )
    text_low = text_first.astype(jnp.bfloat16)
    layout_low = layout_first.astype(jnp.bfloat16)
    text_inputs, layout_inputs = (
        lax.all_gather(text_low, "tensor", axis=0, tiled=True),
        lax.all_gather(layout_low, "tensor", axis=0, tiled=True),
    )
    text_up_w, text_down_w, layout_up_w, layout_down_w = (
        text_upward,
        text_downward,
        layout_upward,
        layout_downward,
    )
    text_hidden = matmul(text_inputs, text_up_w)
    layout_hidden = matmul(layout_inputs, layout_up_w)
    text_active, text_gelu_pull = jax.vjp(gelu_exact, text_hidden)
    layout_active, layout_gelu_pull = jax.vjp(gelu_exact, layout_hidden)
    text_active = text_active.astype(jnp.bfloat16)
    layout_active = layout_active.astype(jnp.bfloat16)
    text_partial = matmul(text_active, text_down_w)
    layout_partial = matmul(layout_active, layout_down_w)
    text_feed, layout_feed = (
        lax.psum_scatter(text_partial, "tensor", scatter_dimension=0, tiled=True),
        lax.psum_scatter(layout_partial, "tensor", scatter_dimension=0, tiled=True),
    )
    text_out, text_pull_two = jax.vjp(
        normalize, text_first + text_feed, text_norms[2], text_norms[3]
    )
    layout_out, layout_pull_two = jax.vjp(
        normalize, layout_first + layout_feed, layout_norms[2], layout_norms[3]
    )
    text_result = text_out.astype(jnp.bfloat16).reshape(pages, slots, width_text)
    layout_result = layout_out.astype(jnp.bfloat16).reshape(pages, slots, width_layout)
    text_dsecond, text_dgain_two, text_dshift_two = text_pull_two(
        text_cotangent.reshape(-1, width_text).astype(jnp.float32)
    )
    layout_dsecond, layout_dgain_two, layout_dshift_two = layout_pull_two(
        layout_cotangent.reshape(-1, width_layout).astype(jnp.float32)
    )
    text_dfeed = text_dsecond.astype(jnp.bfloat16)
    layout_dfeed = layout_dsecond.astype(jnp.bfloat16)
    text_dfeed_all, layout_dfeed_all = (
        lax.all_gather(text_dfeed, "tensor", axis=0, tiled=True),
        lax.all_gather(layout_dfeed, "tensor", axis=0, tiled=True),
    )
    text_dhidden = text_gelu_pull(matmul(text_dfeed_all, text_down_w.T))[0].astype(jnp.bfloat16)
    layout_dhidden = layout_gelu_pull(matmul(layout_dfeed_all, layout_down_w.T))[0].astype(
        jnp.bfloat16
    )
    text_down_grad = matmul(text_active.T, text_dfeed_all)
    layout_down_grad = matmul(layout_active.T, layout_dfeed_all)
    text_up_grad = matmul(text_inputs.T, text_dhidden)
    layout_up_grad = matmul(layout_inputs.T, layout_dhidden)
    text_dinput = matmul(text_dhidden, text_up_w.T)
    layout_dinput = matmul(layout_dhidden, layout_up_w.T)
    text_dinput, layout_dinput = (
        lax.psum_scatter(text_dinput, "tensor", scatter_dimension=0, tiled=True),
        lax.psum_scatter(layout_dinput, "tensor", scatter_dimension=0, tiled=True),
    )
    text_up_grad, text_down_grad, layout_up_grad, layout_down_grad = (
        lax.psum(text_up_grad.astype(jnp.bfloat16), "dp").astype(jnp.float32),
        lax.psum(text_down_grad.astype(jnp.bfloat16), "dp").astype(jnp.float32),
        lax.psum(layout_up_grad.astype(jnp.bfloat16), "dp").astype(jnp.float32),
        lax.psum(layout_down_grad.astype(jnp.bfloat16), "dp").astype(jnp.float32),
    )
    text_dresid, text_dgain_one, text_dshift_one = text_pull_one(text_dsecond + text_dinput)
    layout_dresid, layout_dgain_one, layout_dshift_one = layout_pull_one(
        layout_dsecond + layout_dinput
    )
    text_datt = text_dresid.astype(jnp.bfloat16)
    layout_datt = layout_dresid.astype(jnp.bfloat16)
    text_mix_grad = matmul(text_mixed.T, text_datt)
    layout_mix_grad = matmul(layout_mixed.T, layout_datt)
    text_dmixed = (
        matmul(text_datt, text_mixing.T).astype(jnp.bfloat16).reshape(pages, slots, HEADS, -1)
    )
    layout_dmixed = (
        matmul(layout_datt, layout_mixing.T).astype(jnp.bfloat16).reshape(pages, slots, HEADS, -1)
    )
    text_djoint, layout_djoint = lax.map(
        page_backward,
        (text_grid, layout_grid, page_counts, text_total, layout_total, text_dmixed, layout_dmixed),
    )
    text_djoint = text_djoint.reshape(-1, 3 * width_text)
    layout_djoint = layout_djoint.reshape(-1, 3 * width_layout)
    text_joint_grad = matmul(text_rows.T, text_djoint)
    layout_joint_grad = matmul(layout_rows.T, layout_djoint)
    text_gradient = (text_dresid + matmul(text_djoint, text_joint.T)).reshape(
        pages, slots, width_text
    )
    layout_gradient = (layout_dresid + matmul(layout_djoint, layout_joint.T)).reshape(
        pages, slots, width_layout
    )
    text_norm_grad = jnp.stack([text_dgain_one, text_dshift_one, text_dgain_two, text_dshift_two])
    layout_norm_grad = jnp.stack(
        [layout_dgain_one, layout_dshift_one, layout_dgain_two, layout_dshift_two]
    )
    (
        text_joint_grad,
        text_mix_grad,
        text_norm_grad,
        layout_joint_grad,
        layout_mix_grad,
        layout_norm_grad,
    ) = lax.psum(
        (
            text_joint_grad,
            text_mix_grad,
            text_norm_grad,
            layout_joint_grad,
            layout_mix_grad,
            layout_norm_grad,
        ),
        ("dp", "tensor"),
    )
    return (
        text_result,
        layout_result,
        text_gradient,
        layout_gradient,
        text_joint_grad,
        text_mix_grad,
        text_norm_grad,
        text_up_grad,
        text_down_grad,
        layout_joint_grad,
        layout_mix_grad,
        layout_norm_grad,
        layout_up_grad,
        layout_down_grad,
    )


def solution(mesh):
    return jax.shard_map(
        shards,
        mesh=mesh,
        in_specs=(
            P(("dp", "tensor"), None, None),
            P(("dp", "tensor"), None, None),
            P(("dp", "tensor")),
            P(),
            P(),
            P(),
            P(None, "tensor"),
            P("tensor", None),
            P(),
            P(),
            P(),
            P(None, "tensor"),
            P("tensor", None),
            P(("dp", "tensor"), None, None),
            P(("dp", "tensor"), None, None),
        ),
        out_specs=(
            P(("dp", "tensor"), None, None),
            P(("dp", "tensor"), None, None),
            P(("dp", "tensor"), None, None),
            P(("dp", "tensor"), None, None),
            P(),
            P(),
            P(),
            P(None, "tensor"),
            P("tensor", None),
            P(),
            P(),
            P(),
            P(None, "tensor"),
            P("tensor", None),
        ),
        check_vma=False,
    )
```

profile of v0, /device:TPU:0, one launch (start us, length us, event | category | flops | bytes accessed | tf_op | source)
XLA Modules:
  0.0 606.4 jit_solution(1691573093866012901)
XLA Ops:
  7.2 1.9 copy-done
  9.2 4.5 convolution_convert_fusion
  13.7 4.3 copy.43
  18.0 7.8 %fusion.50 = f32[12,512,512]{1,2,0:T(8,128)} fusion(bf16[512,3,12,64]{0,3,2,1:T(8,128)(2,1)} %bitcast.190), kind=kOutput, calls=%fused_computation.103 | convolution fusion | flops 402653184 | bytes 14155776 | tf_op jit(solution)/shard_map/while/body/eval_jaxpr/qhd,khd->hqk/dot_general | solution.py:22
  26.9 6.8 %fusion.82 = (f32[12,512]{1,0:T(8,128)S(1)}, f32[12,512,512]{1,2,0:T(8,128)S(1)}) fusion(bf16[512,3,12,16]{0,3,2,1:T(8,128)(2,1)S(1)} %bitcast.203, f32[12,512,512]{1,2,0:T(8,128)} %fusion.50, pred[512]{0:T(512)(128)(4,1)S(1)} %iota_compare_fusion), kind=kOutput, calls=%fused_computation.171 | convolution fusion | flops 116385792 | bytes 25584128 | tf_op jit(solution)/shard_map/while/body/eval_jaxpr/qhd,khd->hqk/dot_general | solution.py:22
  33.7 1.9 exponential_reduce_fusion
  35.5 2.6 copy-done.1
  38.2 9.4 %fusion.5 = bf16[12,512,512]{1,2,0:T(8,128)(2,1)} fusion(f32[12,512,512]{1,2,0:T(8,128)} %copy-done.1, f32[12,512]{1,0:T(8,128)S(1)} %log_add_fusion), kind=kLoop, calls=%fused_computation.11 | loop fusion | flops 6291456 | bytes 18898944 | tf_op jit(solution)/shard_map/while/body/eval_jaxpr/convert_element_type | solution.py:41
  47.6 4.1 convolution_convert_fusion.4
  54.5 1.2 fusion.32
  56.0 3.9 convolution_convert_fusion.7
  61.5 2.2 all_gather.13
  63.7 4.8 multiply_convert_fusion.1
  69.4 1.3 fusion.86
  70.9 19.8 %multiply_convert_fusion = (bf16[1024,1536]{1,0:T(8,128)(2,1)S(1)}, f32[1024,1536]{1,0:T(8,128)}, f32[1024,1536]{1,0:T(8,128)}) fusion(bf16[1024,768]{1,0:T(8,128)(2,1)} %all-gather.3.cloned.1.call-done, bf16[768,1536]{1,0:T(8,128)(2,1)} %param.21), kind=kOutput, calls=%fused_computation.14 | convolution fusion | flops 2518155264 | bytes 19660800 | tf_op jit(solution)/shard_map/dot_general | solution.py:93
  90.7 1.7 copy-done.78
  92.4 4.3 fusion.85
  96.7 1.3 fusion.75
  98.8 1.7 fusion.55
  100.5 9.9 %reduce-scatter.5.cloned.1.call-done = f32[512,768]{1,0:T(8,128)} async-done(((f32[1024,768]{1,0:T(8,128)}), f32[512,768]{1,0:T(8,128)}) %reduce-scatter.5.cloned.1.call-update) | async-done | bytes 1572880 | tf_op jit(solution)/shard_map/reduce_scatter | solution.py:155
  110.4 2.5 fusion.78
  113.2 1.3 fusion.24
  114.5 1.6 fusion.74
  116.1 1.1 copy-done.7
  118.3 12.3 %reduce-scatter.11.cloned.1.call-start = ((), (), s32[]{:S(2)}) async-start(), calls=%async_computation.9 | async-start | bytes 1179648 | tf_op jit(solution)/shard_map/reduce_scatter | solution.py:190
  131.3 1.8 fusion.56
  133.2 1.2 add_convert_fusion.8
  134.4 2.1 all_gather.15
  136.5 2.9 add_convert_fusion.2
  140.4 1.3 fusion.88
  141.8 9.9 %add_convert_fusion.1 = bf16[1024,1536]{1,0:T(8,128)(2,1)S(1)} fusion(f32[1024,1536]{1,0:T(8,128)} %get-tuple-element.151, f32[1024,1536]{1,0:T(8,128)} %get-tuple-element.164, bf16[1024,768]{1,0:T(8,128)(2,1)} %all-gather.5.cloned.1.call-done, bf16[1536,768]{1,0:T(8,128)(2,1)} %param.22), kind=kOutput, calls=%fused_computation.13 | convolution fusion | flops 2437939200 | bytes 19660800 | tf_op jit(solution)/shard_map/dot_general | solution.py:93
  151.7 1.7 copy-done.76
  153.4 4.3 fusion.87
  157.8 2.3 convolution_convert_fusion.9
  160.0 2.3 convolution_convert_fusion.8
  162.3 3.0 multiply_reduce_fusion.6
  166.0 1.2 fusion.72
  168.8 5.4 convolution_bitcast_fusion.3
  174.2 7.4 %fusion.62 = f32[12,512,512]{1,2,0:T(8,128)} fusion(bf16[512,12,16]{0,2,1:T(8,128)(2,1)S(1)} %bitcast.211, bf16[512,3,12,16]{0,3,2,1:T(8,128)(2,1)} %bitcast.205), kind=kOutput, calls=%fused_computation.131 | convolution fusion | flops 100663296 | bytes 12976128 | tf_op jit(solution)/shard_map/while/body/eval_jaxpr/qhd,khd->hqk/dot_general | solution.py:59
  181.6 4.0 convolution_convert_fusion.2
  185.6 3.9 convolution_convert_fusion.1
  189.7 3.9 multiply_reduce_fusion.2
  195.4 1.7 convolution_convert_fusion.3
  197.1 2.3 copy.46
  199.5 12.8 %multiply_reduce_fusion.1 = (f32[12,512]{1,0:T(8,128)}, f32[12,512,512]{1,2,0:T(8,128)}) fusion(f32[12,512,512]{1,2,0:T(8,128)} %copy-done.1, f32[12,512]{1,0:T(8,128)} %copy-done.31, bf16[512,12,64]{0,2,1:T(8,128)(2,1)} %bitcast.197, bf16[512,3,12,64]{0,3,2,1:T(8,128)(2,1)} %bitcast.191), kind=kOutput, calls=%fused_computation.5 | convolution fusion | flops 412084224 | bytes 26796032 | tf_op jit(solution)/shard_map/while/body/eval_jaxpr/qhd,khd->hqk/dot_general | solution.py:59
  212.2 22.8 %fusion.43 = bf16[512,1,12,16]{0,3,2,1:T(8,128)(2,1)} fusion(f32[12,512,512]{1,2,0:T(8,128)} %fusion.62, f32[12,512,512]{1,2,0:T(8,128)} %get-tuple-element.169, f32[12,512,512]{1,2,0:T(8,128)} %copy-done.1, f32[12,512]{1,0:T(8,128)} %get-tuple-element.168, f32[12,512]{1,0:T(8,128)} %copy-done.31, bf16[512,3,12,16]{0,3,2,1:T(8,128)(2,1)} %bitcast.206), kind=kOutput, calls=%fused_computation.90 | convolution fusion | flops 129178112 | bytes 63406080 | tf_op jit(solution)/shard_map/while/body/eval_jaxpr/hqk,qhd->khd/dot_general | solution.py:71
  235.0 22.6 %fusion.37 = bf16[512,1,12,16]{0,3,2,1:T(8,128)(2,1)} fusion(f32[12,512,512]{1,2,0:T(8,128)} %fusion.62, f32[12,512,512]{1,2,0:T(8,128)} %get-tuple-element.169, f32[12,512,512]{1,2,0:T(8,128)} %copy-done.1, f32[12,512]{1,0:T(8,128)} %get-tuple-element.168, f32[12,512]{1,0:T(8,128)} %copy-done.31, bf16[512,3,12,16]{0,3,2,1:T(8,128)(2,1)} %bitcast.207), kind=kOutput, calls=%fused_computation.88 | convolution fusion | flops 129178112 | bytes 63406080 | tf_op jit(solution)/shard_map/while/body/eval_jaxpr/hqk,khd->qhd/dot_general | solution.py:67
  257.6 1.2 maximum_convert_fusion.1
  258.9 5.3 convolution_bitcast_fusion.1
  264.2 10.0 %fusion.2 = bf16[12,512,512]{1,2,0:T(8,128)(2,1)S(1)} fusion(f32[12,512,512]{1,2,0:T(8,128)} %get-tuple-element.169, f32[12,512,512]{1,2,0:T(8,128)} %copy-done.1, f32[12,512]{1,0:T(8,128)S(1)} %copy-done.42, f32[12,512]{1,0:T(8,128)S(1)} %copy-done.32), kind=kLoop, calls=%fused_computation.9 | loop fusion | flops 12582912 | bytes 31506432 | tf_op jit(solution)/shard_map/while/body/eval_jaxpr/convert_element_type | solution.py:84
  274.3 2.0 multiply_bitcast_fusion
  278.4 1.2 convolution_bitcast_fusion.2
  280.3 2.3 fusion.70
  282.6 5.0 convolution_bitcast_fusion
  287.6 1.3 convert_reduce_fusion
  291.8 86.3 %all-reduce.8.cloned.1.call-done = (bf16[768,1536]{1,0:T(8,128)(2,1)}, bf16[1536,768]{1,0:T(8,128)(2,1)}, bf16[192,384]{1,0:T(8,128)(2,1)}, bf16[384,192]{0,1:T(8,128)(2,1)}) async-done(((bf16[768,1536]{1,0:T(8,128)(2,1)}, bf16[1536,768]{1,0:T(8,128)(2,1)}, bf16[192,384]{1,0:T(8,128)(2,1)}, bf16[384,192]{0,1:T(8,128)(2,1)}), (bf16[768,1536]{1,0:T(8,128)(2,1)}, bf16[1536,768]{1,0:T(8,128)(2,1)}, ...) | async-done | bytes 5013520 | tf_op jit(solution)/shard_map/psum | solution.py:193
  378.2 4.6 convert_element_type.188
  382.9 2.5 convert_element_type.190
  387.0 41.7 %all-reduce = (f32[4,768]{1,0:T(4,128)}, f32[4,192]{1,0:T(4,128)}) all-reduce(f32[4,768]{1,0:T(4,128)S(1)} %pad_maximum_fusion, f32[4,192]{1,0:T(4,128)} %pad_maximum_fusion.1), channel_id=1, replica_groups=mesh['dp'=16,'tensor'=2] {'dp','tensor'}, use_global_device_ids=true, to_apply=%region_30.31 | all-reduce | flops 3840 | bytes 30720 | tf_op jit(solution)/shard_map/psum | solution.py:237
  428.7 2.3 fusion.33
  431.0 5.5 add_bitcast_fusion
  436.5 149.9 %all-reduce.6.cloned.1.call-done = (f32[768,2304]{0,1:T(8,128)}, f32[768,768]{1,0:T(8,128)}, f32[192,576]{1,0:T(8,128)}, f32[192,192]{1,0:T(8,128)}) async-done(((f32[768,2304]{0,1:T(8,128)}, f32[768,768]{1,0:T(8,128)}, f32[192,576]{1,0:T(8,128)}, f32[192,192]{1,0:T(8,128)}), (f32[768,2304]{0,1:T(8,128)}, f32[768,768]{1,0:T(8,128)}, f32[192,576]{1,0:T(8,128)}, ...) | async-done | bytes 10027024 | tf_op jit(solution)/shard_map/psum | solution.py:237
  586.4 8.0 %copy.53 = f32[768,2304]{1,0:T(8,128)} copy(f32[768,2304]{0,1:T(8,128)} %get-tuple-element.128) | data formatting | bytes 14155776
  594.3 3.3 copy.71
  (218 shorter events, 22.8 us)
Async XLA Ops:
  7.2 63.6 %all-gather.3.cloned.1.call-start = ((), (), s32[]{:S(2)}) async-start(), calls=%async_computation.4 | async-start | bytes 2359296 | tf_op jit(solution)/shard_map/all_gather | solution.py:137
  18.0 8.5 %copy-start.23 = (bf16[1,512,192]{1,2,0:T(8,128)(2,1)S(1)}, bf16[1,512,192]{1,2,0:T(8,128)(2,1)}, u32[]{:S(2)}) copy-start(bf16[1,512,192]{1,2,0:T(8,128)(2,1)} %param.16) | copy-start | bytes 589828
  18.0 8.5 %copy-start.28 = (bf16[192,576]{1,0:T(8,128)(2,1)S(1)}, bf16[192,576]{1,0:T(8,128)(2,1)}, u32[]{:S(2)}) copy-start(bf16[192,576]{1,0:T(8,128)(2,1)} %param.23) | copy-start | bytes 663556
  26.8 6.8 %copy-start.17 = (bf16[512,576]{0,1:T(8,128)(2,1)}, bf16[512,576]{0,1:T(8,128)(2,1)S(1)}, u32[]{:S(2)}) copy-start(bf16[512,576]{0,1:T(8,128)(2,1)S(1)} %convolution_convert_fusion.5) | copy-start | bytes 1769476
  33.7 4.5 copy-start.1
  38.2 9.4 %copy-start.31 = (f32[12,512]{1,0:T(8,128)}, f32[12,512]{1,0:T(8,128)S(1)}, u32[]{:S(2)}) copy-start(f32[12,512]{1,0:T(8,128)S(1)} %log_add_fusion) | copy-start | bytes 73732
  38.2 9.4 %copy-start.4 = (bf16[512,2304]{0,1:T(8,128)(2,1)S(1)}, bf16[512,2304]{0,1:T(8,128)(2,1)}, u32[]{:S(2)}) copy-start(bf16[512,2304]{0,1:T(8,128)(2,1)} %copy.43) | copy-start | bytes 7077892
  47.6 4.1 copy-start.61
  47.6 4.8 copy-start.29
  47.6 4.8 copy-start.74
  55.7 41.0 %reduce-scatter.7.cloned.1.call-start = ((), (), s32[]{:S(2)}) async-start(), calls=%async_computation.6 | async-start | bytes 1179648 | tf_op jit(solution)/shard_map/reduce_scatter | solution.py:156
  56.0 3.9 copy-start.24
  56.0 3.9 copy-start.34
  56.0 4.3 copy-start.69
  59.9 8.6 %copy-start.20 = (bf16[12,512,16]{1,2,0:T(8,128)(2,1)}, bf16[12,512,16]{1,2,0:T(8,128)(2,1)S(1)}, u32[]{:S(2)}) copy-start(bf16[12,512,16]{1,2,0:T(8,128)(2,1)S(1)} %convolution_convert_fusion.7) | copy-start | bytes 589828
  59.9 3.8 copy-start.40
  63.7 4.8 copy-start.26
  63.7 5.7 copy-start.39
  70.8 39.6 %reduce-scatter.5.cloned.1.call-start = ((), (), s32[]{:S(2)}) async-start(), calls=%async_computation.5 | async-start | bytes 4718592 | tf_op jit(solution)/shard_map/reduce_scatter | solution.py:155
  70.8 21.5 %copy-start.70 = (bf16[1536,768]{1,0:T(8,128)(2,1)S(1)}, bf16[1536,768]{1,0:T(8,128)(2,1)}, u32[]{:S(2)}) copy-start(bf16[1536,768]{1,0:T(8,128)(2,1)} %param.22) | copy-start | bytes 7077892
  96.7 45.1 %all-gather.5.cloned.1.call-start = ((), (), s32[]{:S(2)}) async-start(), calls=%async_computation.7 | async-start | bytes 2359296 | tf_op jit(solution)/shard_map/all_gather | solution.py:175
  110.3 2.8 copy-start.10
  110.3 2.8 copy-start.45
  118.3 44.1 %reduce-scatter.11.cloned.1.call-start = ((), (), s32[]{:S(2)}) async-start(), calls=%async_computation.9 | async-start | bytes 1179648 | tf_op jit(solution)/shard_map/reduce_scatter | solution.py:190
  131.3 5.1 copy-start.49
  131.3 5.1 copy-start.50
  133.2 3.3 copy-start.56
  136.5 3.0 copy-start.27
  136.5 3.9 copy-start.41
  141.7 47.9 %reduce-scatter.9.cloned.1.call-start = ((), (), s32[]{:S(2)}) async-start(), calls=%async_computation.8 | async-start | bytes 4718592 | tf_op jit(solution)/shard_map/reduce_scatter | solution.py:189
  141.8 11.6 %copy-start.71 = (bf16[768,1536]{1,0:T(8,128)(2,1)S(1)}, bf16[768,1536]{1,0:T(8,128)(2,1)}, u32[]{:S(2)}) copy-start(bf16[768,1536]{1,0:T(8,128)(2,1)} %param.21) | copy-start | bytes 7077892
  157.7 220.5 %all-reduce.8.cloned.1.call-start = ((), (), s32[]{:S(2)}) async-start(), calls=%async_computation.11 | async-start | bytes 10027008 | tf_op jit(solution)/shard_map/psum | solution.py:193
  162.3 4.9 copy-start.35
  162.3 5.6 copy-start.21
  167.2 7.0 %copy-start.47 = (f32[512]{0:T(512)}, f32[512]{0:T(512)S(1)}, u32[]{:S(2)}) copy-start(f32[512]{0:T(512)S(1)} %negate_multiply_fusion.2) | copy-start | bytes 6148
  174.2 7.4 %copy-start.72 = (bf16[1024,768]{1,0:T(8,128)(2,1)S(1)}, bf16[1024,768]{1,0:T(8,128)(2,1)}, u32[]{:S(2)}) copy-start(bf16[1024,768]{1,0:T(8,128)(2,1)} %all-gather.3.cloned.1.call-done) | copy-start | bytes 4718596
  174.2 7.4 %copy-start.77 = (bf16[1024,1536]{1,0:T(8,128)(2,1)S(1)}, bf16[1024,1536]{1,0:T(8,128)(2,1)}, u32[]{:S(2)}) copy-start(bf16[1024,1536]{1,0:T(8,128)(2,1)} %copy-done.76) | copy-start | bytes 9437188
  181.6 4.0 copy-start.73
  181.6 4.0 copy-start.79
  189.6 4.0 copy-start.53
  189.6 396.8 %all-reduce.6.cloned.1.call-start = ((), (), s32[]{:S(2)}) async-start(), calls=%async_computation.10 | async-start | bytes 20250624 | tf_op jit(solution)/shard_map/psum | solution.py:237
  189.6 3.9 copy-start.3
  194.3 85.3 %copy-start.65 = (f32[512]{0:T(512)}, f32[512]{0:T(512)S(1)}, u32[]{:S(2)}) copy-start(f32[512]{0:T(512)S(1)} %negate_multiply_fusion.4) | copy-start | bytes 6148
  258.9 18.9 %copy-start.16 = (bf16[512,3,12,16]{0,3,2,1:T(8,128)(2,1)}, bf16[512,3,12,16]{0,3,2,1:T(8,128)(2,1)S(1)}, u32[]{:S(2)}) copy-start(bf16[512,3,12,16]{0,3,2,1:T(8,128)(2,1)S(1)} %maximum_convert_fusion.1) | copy-start | bytes 1769476
  258.9 5.3 copy-start.32
  258.9 5.3 copy-start.42
  264.2 10.1 %copy-start.5 = (bf16[512,2304]{0,1:T(8,128)(2,1)S(1)}, bf16[512,2304]{0,1:T(8,128)(2,1)}, u32[]{:S(2)}) copy-start(bf16[512,2304]{0,1:T(8,128)(2,1)} %copy.43) | copy-start | bytes 7077892
  277.5 2.8 copy-start.14
  277.7 4.8 copy-start.8
  280.3 2.3 copy-start.30
  287.6 3.0 copy-start.66
  287.6 3.0 copy-start.67
  287.6 3.0 copy-start.68
  287.6 3.6 copy-start.58
  378.2 4.7 copy-start.22
  382.8 2.6 copy-start.38
  382.8 3.3 copy-start.37
  382.8 4.1 copy-start.60
  382.8 4.1 copy-start.59
  382.8 4.1 copy-start.62
  382.8 4.1 copy-start.63
  382.9 45.8 %copy-start.48 = (f32[512]{0:T(512)S(1)}, f32[512]{0:T(512)}, u32[]{:S(2)}) copy-start(f32[512]{0:T(512)} %copy-done.47) | copy-start | bytes 6148
  594.3 3.3 copy-start.33
  594.3 4.1 copy-start.36
  (24 other events, 28.6 us)
Sparse Core Ops, SparseCore 0:
  55.8 12.4 all-gather.2
  70.9 10.8 reduce-scatter.6
  96.8 13.5 reduce-scatter.4
  118.4 10.9 all-gather.4
  141.8 9.3 reduce-scatter.10
  157.8 12.0 reduce-scatter.8
  189.7 188.4 all-reduce.7
  385.7 200.6 all-reduce.5
where the time goes:
time: 616 us; the launch traced here: 606 us
  waiting for transfers between devices  246 us (40%)
  matrix products  188 us (31%)
  other arithmetic  58.9 us (10%)
  blocking collectives  45.9 us (7%)
  local copies, waits for them, and re-layouts  37.9 us (6%)
  between operations  16.1 us (3%)
  starting transfers between devices  12.9 us (2%)
    psum x1, waiting for transfers between devices, shards(): lax.psum((text_joint_grad, text_mix_grad, text_norm_grad, layout_joint_gr...  150 us
    dot_general x24, matrix products, matmul(): return jnp.dot(left, right, preferred_element_type=jnp.float32)  86.4 us
    psum x1, waiting for transfers between devices, shards(): lax.psum(text_up_grad.astype(jnp.bfloat16), 'dp').astype(jnp.float32)  86.3 us
    psum x1, blocking collectives, shards(): lax.psum((text_joint_grad, text_mix_grad, text_norm_grad, layout_joint_gr...  41.7 us
    unnamed x164, local copies, waits for them, and re-layouts  28.8 us
    dot_general x2, matrix products, joint_grads(): jnp.einsum('hqk,qhd->khd', score_grad, grid[:, 0], preferred_element_type...  24.8 us
    dot_general x2, matrix products, joint_grads(): jnp.einsum('hqk,khd->qhd', score_grad, grid[:, 1], preferred_element_type...  23.8 us
    dot_general x2, matrix products, probs_back(): jnp.einsum('qhd,khd->hqk', upstream, values, preferred_element_type=jnp.f...  20.2 us
  transfers between devices with their start and end apart: 8, of which 3 were waited for; matrix products, arithmetic and copies ran while one was open for 34% of the time, Pallas kernels for 0%

commit v1 on v0

--- a/solution.py
+++ b/solution.py
@@ -235,15 +235,18 @@
         layout_mix_grad,
         layout_norm_grad,
     ) = lax.psum(
-        (
-            text_joint_grad,
-            text_mix_grad,
-            text_norm_grad,
-            layout_joint_grad,
-            layout_mix_grad,
-            layout_norm_grad,
+        lax.psum(
+            (
+                text_joint_grad,
+                text_mix_grad,
+                text_norm_grad,
+                layout_joint_grad,
+                layout_mix_grad,
+                layout_norm_grad,
+            ),
+            "tensor",
         ),
-        ("dp", "tensor"),
+        "dp",
     )
     return (
         text_result,

time: 616 us -> 845 us (1.37)
  waiting for transfers between devices: 246 us -> 439 us
  blocking collectives: 45.9 us -> 87.6 us
    psum x0 -> x1, waiting for transfers between devices: none -> 207 us  [shards(): lax.psum(lax.psum((text_joint_grad, text_mix_grad, text_norm_grad, layout...]
    psum x1, waiting for transfers between devices: 150 us -> 28.8 us  [shards(): lax.psum((text_joint_grad, text_mix_grad, text_norm_grad, layout_joint_gr...]
    psum x1, waiting for transfers between devices: 86.3 us -> 193 us  [shards(): lax.psum(text_up_grad.astype(jnp.bfloat16), 'dp').astype(jnp.float32)]
    psum x0 -> x1, blocking collectives: none -> 78.8 us  [shards(): lax.psum(lax.psum((text_joint_grad, text_mix_grad, text_norm_grad, layout...]
    psum x1, blocking collectives: 41.7 us -> 4.57 us  [shards(): lax.psum((text_joint_grad, text_mix_grad, text_norm_grad, layout_joint_gr...]
    unnamed x164 -> x178, local copies, waits for them, and re-layouts: 28.8 us -> 29.6 us
  transfers between devices with their start and end apart: 8 -> 9, of which waited for: 3 -> 4; matrix products, arithmetic and copies ran while one was open for 34% -> 14% of each run, Pallas kernels for 0% -> 0%
where the time goes in v1:
time: 845 us; the launch traced here: 836 us
  waiting for transfers between devices  439 us (52%)
  matrix products  191 us (23%)
  blocking collectives  87.6 us (10%)
  other arithmetic  54.5 us (6%)
  local copies, waits for them, and re-layouts  38.7 us (5%)
  between operations  15.8 us (2%)
  starting transfers between devices  9.79 us (1%)
    psum x1, waiting for transfers between devices, shards(): lax.psum(lax.psum((text_joint_grad, text_mix_grad, text_norm_grad, layout...  207 us
    psum x1, waiting for transfers between devices, shards(): lax.psum(text_up_grad.astype(jnp.bfloat16), 'dp').astype(jnp.float32)  193 us
    dot_general x24, matrix products, matmul(): return jnp.dot(left, right, preferred_element_type=jnp.float32)  90.2 us
    psum x1, blocking collectives, shards(): lax.psum(lax.psum((text_joint_grad, text_mix_grad, text_norm_grad, layout...  78.8 us
    unnamed x178, local copies, waits for them, and re-layouts  29.6 us
    psum x1, waiting for transfers between devices, shards(): lax.psum((text_joint_grad, text_mix_grad, text_norm_grad, layout_joint_gr...  28.8 us
    dot_general x2, matrix products, joint_grads(): jnp.einsum('hqk,qhd->khd', score_grad, grid[:, 0], preferred_element_type...  24.8 us
    dot_general x2, matrix products, joint_grads(): jnp.einsum('hqk,khd->qhd', score_grad, grid[:, 1], preferred_element_type...  23.9 us
  transfers between devices with their start and end apart: 9, of which 4 were waited for; matrix products, arithmetic and copies ran while one was open for 14% of the time, Pallas kernels for 0%

profile of v1, /device:TPU:0, one launch (start us, length us, event | category | flops | bytes accessed | tf_op | source)
XLA Modules:
  0.0 836.1 jit_solution(6863856620969130872)
XLA Ops:
  7.2 1.9 copy-done
  9.2 4.5 convolution_convert_fusion
  13.7 4.3 copy.43
  18.0 7.8 fusion.50
  26.9 6.8 fusion.82
  33.7 1.9 exponential_reduce_fusion
  35.6 2.7 copy-done.1
  38.3 9.4 %fusion.5 = bf16[12,512,512]{1,2,0:T(8,128)(2,1)} fusion(f32[12,512,512]{1,2,0:T(8,128)} %copy-done.1, f32[12,512]{1,0:T(8,128)S(1)} %log_add_fusion), kind=kLoop, calls=%fused_computation.11 | loop fusion | flops 6291456 | bytes 18898944 | tf_op jit(solution)/shard_map/while/body/eval_jaxpr/convert_element_type | solution.py:41
  47.7 4.0 convolution_convert_fusion.4
  54.5 1.2 fusion.32
  56.1 3.9 convolution_convert_fusion.7
  61.5 2.1 all_gather.13
  63.7 4.8 multiply_convert_fusion.1
  69.4 1.3 fusion.86
  70.9 19.7 %multiply_convert_fusion = (bf16[1024,1536]{1,0:T(8,128)(2,1)S(1)}, f32[1024,1536]{1,0:T(8,128)}, f32[1024,1536]{1,0:T(8,128)}) fusion(bf16[1024,768]{1,0:T(8,128)(2,1)} %all-gather.3.cloned.1.call-done, bf16[768,1536]{1,0:T(8,128)(2,1)} %param.21), kind=kOutput, calls=%fused_computation.14 | convolution fusion | flops 2518155264 | bytes 19660800 | tf_op jit(solution)/shard_map/dot_general | solution.py:93
  90.5 1.6 copy-done.82
  92.1 4.3 fusion.85
  96.5 1.3 fusion.75
  98.6 1.6 fusion.55
  100.2 9.9 %reduce-scatter.5.cloned.1.call-done = f32[512,768]{1,0:T(8,128)} async-done(((f32[1024,768]{1,0:T(8,128)}), f32[512,768]{1,0:T(8,128)}) %reduce-scatter.5.cloned.1.call-update) | async-done | bytes 1572880 | tf_op jit(solution)/shard_map/reduce_scatter | solution.py:155
  110.1 2.5 fusion.78
  113.0 1.3 fusion.24
  114.3 1.6 fusion.74
  118.1 9.2 %reduce-scatter.11.cloned.1.call-start = ((), (), s32[]{:S(2)}) async-start(), calls=%async_computation.9 | async-start | bytes 1179648 | tf_op jit(solution)/shard_map/reduce_scatter | solution.py:190
  128.0 1.8 fusion.56
  129.8 1.2 add_convert_fusion.8
  131.0 2.1 all_gather.15
  133.1 2.9 add_convert_fusion.2
  137.0 1.3 fusion.88
  138.4 9.9 %add_convert_fusion.1 = bf16[1024,1536]{1,0:T(8,128)(2,1)S(1)} fusion(f32[1024,1536]{1,0:T(8,128)} %get-tuple-element.157, f32[1024,1536]{1,0:T(8,128)} %get-tuple-element.170, bf16[1024,768]{1,0:T(8,128)(2,1)} %all-gather.5.cloned.1.call-done, bf16[1536,768]{1,0:T(8,128)(2,1)} %param.22), kind=kOutput, calls=%fused_computation.13 | convolution fusion | flops 2437939200 | bytes 19660800 | tf_op jit(solution)/shard_map/dot_general | solution.py:93
  148.4 1.7 copy-done.81
  150.0 4.3 fusion.87
  154.5 3.0 multiply_reduce_fusion.6
  158.1 1.2 fusion.72
  161.0 6.0 convolution_bitcast_fusion.3
  167.0 7.2 fusion.62
  174.2 3.9 multiply_reduce_fusion.2
  180.0 1.7 convolution_convert_fusion.3
  181.7 2.3 copy.46
  184.0 6.1 convolution_bitcast_fusion.1
  190.1 10.4 %multiply_reduce_fusion.1 = (f32[12,512]{1,0:T(8,128)S(1)}, f32[12,512,512]{1,2,0:T(8,128)}) fusion(f32[12,512,512]{1,2,0:T(8,128)} %copy-done.1, f32[12,512]{1,0:T(8,128)S(1)} %copy-done.35, bf16[512,12,64]{0,2,1:T(8,128)(2,1)S(1)} %bitcast.200, bf16[512,3,12,64]{0,3,2,1:T(8,128)(2,1)S(1)} %bitcast.194), kind=kOutput, calls=%fused_computation.5 | convolution fusion | flops 412084224 | bytes 26796032 | tf_op jit(solution)/shard_map/while/body/eval_jaxpr/qhd,khd->hqk/dot_general | solution.py:59
  201.0 6.8 fusion.2
  207.9 2.9 multiply_bitcast_fusion
  210.8 2.0 multiply_bitcast_fusion.1
  212.8 21.9 %fusion.43 = bf16[512,1,12,16]{0,3,2,1:T(8,128)(2,1)} fusion(f32[12,512,512]{1,2,0:T(8,128)} %fusion.62, f32[12,512,512]{1,2,0:T(8,128)} %get-tuple-element.175, f32[12,512,512]{1,2,0:T(8,128)} %copy-done.1, f32[12,512]{1,0:T(8,128)} %copy-done.47, f32[12,512]{1,0:T(8,128)} %copy-done.34, bf16[512,3,12,16]{0,3,2,1:T(8,128)(2,1)} %bitcast.208), kind=kOutput, calls=%fused_computation.90 | convolution fusion | flops 129178112 | bytes 63406080 | tf_op jit(solution)/shard_map/while/body/eval_jaxpr/hqk,qhd->khd/dot_general | solution.py:71
  234.7 21.9 %fusion.37 = bf16[512,1,12,16]{0,3,2,1:T(8,128)(2,1)} fusion(f32[12,512,512]{1,2,0:T(8,128)} %fusion.62, f32[12,512,512]{1,2,0:T(8,128)} %get-tuple-element.175, f32[12,512,512]{1,2,0:T(8,128)} %copy-done.1, f32[12,512]{1,0:T(8,128)} %copy-done.47, f32[12,512]{1,0:T(8,128)} %copy-done.34, bf16[512,3,12,16]{0,3,2,1:T(8,128)(2,1)} %bitcast.209), kind=kOutput, calls=%fused_computation.88 | convolution fusion | flops 129178112 | bytes 63406080 | tf_op jit(solution)/shard_map/while/body/eval_jaxpr/hqk,khd->qhd/dot_general | solution.py:67
  256.7 4.1 fusion.70
  261.9 5.0 convolution_bitcast_fusion
  269.1 2.4 convolution_convert_fusion.9
  271.5 2.3 convolution_convert_fusion.8
  273.8 6.2 convolution_convert_fusion.2
  280.0 3.9 convolution_convert_fusion.1
  284.0 28.8 %all-reduce.11.cloned.1.call-done = (f32[768,2304]{0,1:T(8,128)}, f32[768,768]{1,0:T(8,128)}, f32[192,576]{1,0:T(8,128)}, f32[192,192]{1,0:T(8,128)}) async-done(((f32[768,2304]{0,1:T(8,128)}, f32[768,768]{1,0:T(8,128)}, f32[192,576]{1,0:T(8,128)}, f32[192,192]{1,0:T(8,128)}), (f32[768,2304]{0,1:T(8,128)}, f32[768,768]{1,0:T(8,128)}, f32[192,576]{1,0:T(8,128)}, ...) | async-done | bytes 10027024 | tf_op jit(solution)/shard_map/psum | solution.py:238
  312.8 1.3 convert_reduce_fusion
  317.0 192.9 %all-reduce.13.cloned.1.call-done = (bf16[768,1536]{1,0:T(8,128)(2,1)}, bf16[1536,768]{1,0:T(8,128)(2,1)}, bf16[192,384]{1,0:T(8,128)(2,1)}, bf16[384,192]{0,1:T(8,128)(2,1)}) async-done(((bf16[768,1536]{1,0:T(8,128)(2,1)}, bf16[1536,768]{1,0:T(8,128)(2,1)}, bf16[192,384]{1,0:T(8,128)(2,1)}, bf16[384,192]{0,1:T(8,128)(2,1)}), (bf16[768,1536]{1,0:T(8,128)(2,1)}, bf16[1536,768]{1,0:T(8,128)(2,1)}, ...) | async-done | bytes 5013520 | tf_op jit(solution)/shard_map/psum | solution.py:193
  509.9 4.6 convert_element_type.188
  514.6 2.5 convert_element_type.190
  518.7 4.6 all-reduce.2
  523.3 78.8 %all-reduce = (f32[4,768]{1,0:T(4,128)}, f32[4,192]{1,0:T(4,128)}) all-reduce(f32[4,768]{1,0:T(4,128)} %get-tuple-element.132, f32[4,192]{1,0:T(4,128)} %get-tuple-element.133), channel_id=1, replica_groups=mesh['dp'=16,'tensor'=2] {'dp'}, use_global_device_ids=true, to_apply=%region_33.34 | all-reduce | flops 3840 | bytes 30720 | tf_op jit(solution)/shard_map/psum | solution.py:237
  602.1 2.3 fusion.33
  604.4 5.4 add_bitcast_fusion
  609.7 206.6 %all-reduce.9.cloned.1.call-done = (f32[768,2304]{0,1:T(8,128)}, f32[768,768]{1,0:T(8,128)}, f32[192,576]{1,0:T(8,128)}, f32[192,192]{1,0:T(8,128)}) async-done(((f32[768,2304]{0,1:T(8,128)}, f32[768,768]{1,0:T(8,128)}, f32[192,576]{1,0:T(8,128)}, f32[192,192]{1,0:T(8,128)}), (f32[768,2304]{0,1:T(8,128)}, f32[768,768]{1,0:T(8,128)}, f32[192,576]{1,0:T(8,128)}, ...) | async-done | bytes 10027024 | tf_op jit(solution)/shard_map/psum | solution.py:237
  816.4 8.0 copy.53
  824.3 3.3 copy.75
  (237 shorter events, 25.0 us)
Async XLA Ops:
  7.2 63.6 %all-gather.3.cloned.1.call-start = ((), (), s32[]{:S(2)}) async-start(), calls=%async_computation.4 | async-start | bytes 2359296 | tf_op jit(solution)/shard_map/all_gather | solution.py:137
  18.0 8.5 %copy-start.25 = (bf16[1,512,192]{1,2,0:T(8,128)(2,1)S(1)}, bf16[1,512,192]{1,2,0:T(8,128)(2,1)}, u32[]{:S(2)}) copy-start(bf16[1,512,192]{1,2,0:T(8,128)(2,1)} %param.16) | copy-start | bytes 589828
  18.0 8.5 %copy-start.30 = (bf16[192,576]{1,0:T(8,128)(2,1)S(1)}, bf16[192,576]{1,0:T(8,128)(2,1)}, u32[]{:S(2)}) copy-start(bf16[192,576]{1,0:T(8,128)(2,1)} %param.23) | copy-start | bytes 663556
  26.9 6.8 copy-start.16
  33.7 4.5 copy-start.1
  38.2 9.4 %copy-start.34 = (f32[12,512]{1,0:T(8,128)}, f32[12,512]{1,0:T(8,128)S(1)}, u32[]{:S(2)}) copy-start(f32[12,512]{1,0:T(8,128)S(1)} %log_add_fusion) | copy-start | bytes 73732
  38.3 9.4 %copy-start.4 = (bf16[512,2304]{0,1:T(8,128)(2,1)S(1)}, bf16[512,2304]{0,1:T(8,128)(2,1)}, u32[]{:S(2)}) copy-start(bf16[512,2304]{0,1:T(8,128)(2,1)} %copy.43) | copy-start | bytes 7077892
  47.7 4.1 copy-start.66
  47.7 4.8 copy-start.32
  47.7 4.8 copy-start.79
  55.7 40.8 %reduce-scatter.7.cloned.1.call-start = ((), (), s32[]{:S(2)}) async-start(), calls=%async_computation.6 | async-start | bytes 1179648 | tf_op jit(solution)/shard_map/reduce_scatter | solution.py:156
  56.0 3.9 copy-start.26
  56.0 3.9 copy-start.37
  56.1 4.3 copy-start.74
  59.9 8.5 %copy-start.22 = (bf16[12,512,16]{1,2,0:T(8,128)(2,1)}, bf16[12,512,16]{1,2,0:T(8,128)(2,1)S(1)}, u32[]{:S(2)}) copy-start(bf16[12,512,16]{1,2,0:T(8,128)(2,1)S(1)} %convolution_convert_fusion.7) | copy-start | bytes 589828
  60.0 3.7 copy-start.45
  63.7 4.8 copy-start.28
  63.7 5.7 copy-start.44
  70.8 39.4 %reduce-scatter.5.cloned.1.call-start = ((), (), s32[]{:S(2)}) async-start(), calls=%async_computation.5 | async-start | bytes 4718592 | tf_op jit(solution)/shard_map/reduce_scatter | solution.py:155
  70.8 21.3 %copy-start.75 = (bf16[1536,768]{1,0:T(8,128)(2,1)S(1)}, bf16[1536,768]{1,0:T(8,128)(2,1)}, u32[]{:S(2)}) copy-start(bf16[1536,768]{1,0:T(8,128)(2,1)} %param.22) | copy-start | bytes 7077892
  96.4 42.0 %all-gather.5.cloned.1.call-start = ((), (), s32[]{:S(2)}) async-start(), calls=%async_computation.7 | async-start | bytes 2359296 | tf_op jit(solution)/shard_map/all_gather | solution.py:175
  118.1 36.4 %reduce-scatter.11.cloned.1.call-start = ((), (), s32[]{:S(2)}) async-start(), calls=%async_computation.9 | async-start | bytes 1179648 | tf_op jit(solution)/shard_map/reduce_scatter | solution.py:190
  128.0 5.1 copy-start.54
  128.0 5.1 copy-start.55
  129.8 3.3 copy-start.61
  133.1 3.9 copy-start.46
  138.3 35.9 %reduce-scatter.9.cloned.1.call-start = ((), (), s32[]{:S(2)}) async-start(), calls=%async_computation.8 | async-start | bytes 4718592 | tf_op jit(solution)/shard_map/reduce_scatter | solution.py:189
  138.4 11.6 %copy-start.76 = (bf16[768,1536]{1,0:T(8,128)(2,1)S(1)}, bf16[768,1536]{1,0:T(8,128)(2,1)}, u32[]{:S(2)}) copy-start(bf16[768,1536]{1,0:T(8,128)(2,1)} %param.21) | copy-start | bytes 7077892
  154.4 158.4 %all-reduce.11.cloned.1.call-start = ((), (), s32[]{:S(2)}) async-start(), calls=%async_computation.11 | async-start | bytes 20250624 | tf_op jit(solution)/shard_map/psum | solution.py:238
  154.4 4.9 copy-start.38
  154.4 5.6 copy-start.23
  159.3 7.7 copy-start.52
  174.2 3.9 copy-start.58
  174.2 3.9 copy-start.3
  178.8 77.8 %copy-start.70 = (f32[512]{0:T(512)}, f32[512]{0:T(512)S(1)}, u32[]{:S(2)}) copy-start(f32[512]{0:T(512)S(1)} %negate_multiply_fusion.4) | copy-start | bytes 6148
  184.0 6.1 copy-start.5
  184.0 6.1 copy-start.10
  184.0 6.1 copy-start.35
  184.0 16.5 %slice-start = ((s8[12582912]{0:T(1024)(128)(4,1)}), s8[4194304]{0:T(1024)(128)(4,1)S(1)}, s32[]{:S(2)}) async-start(s8[12582912]{0:T(1024)(128)(4,1)} %bitcast.190), calls=%async_computation.13 | async-start | bytes 8388608
  190.0 10.4 %slice-start.1 = ((s8[12582912]{0:T(1024)(128)(4,1)}), s8[4194304]{0:T(1024)(128)(4,1)S(1)}, s32[]{:S(2)}) async-start(s8[12582912]{0:T(1024)(128)(4,1)} %bitcast.190), calls=%async_computation.14 | async-start | bytes 8388608
  190.1 11.0 %slice-start.2 = ((s8[12582912]{0:T(1024)(128)(4,1)}), s8[4194304]{0:T(1024)(128)(4,1)S(1)}, s32[]{:S(2)}) async-start(s8[12582912]{0:T(1024)(128)(4,1)} %bitcast.190), calls=%async_computation.15 | async-start | bytes 8388608
  200.4 7.4 copy-start.47
  256.6 4.1 copy-start.19
  256.7 4.1 copy-start.20
  256.7 4.1 copy-start.21
  261.1 5.9 copy-start.8
  261.9 5.1 copy-start.31
  261.9 5.1 copy-start.39
  261.9 5.1 copy-start.40
  261.9 5.9 copy-start.27
  269.0 240.8 %all-reduce.13.cloned.1.call-start = ((), (), s32[]{:S(2)}) async-start(), calls=%async_computation.12 | async-start | bytes 10027008 | tf_op jit(solution)/shard_map/psum | solution.py:193
  269.1 4.7 copy-start.77
  273.8 6.2 copy-start.78
  273.8 6.2 copy-start.83
  284.0 532.4 %all-reduce.9.cloned.1.call-start = ((), (), s32[]{:S(2)}) async-start(), calls=%async_computation.10 | async-start | bytes 20250624 | tf_op jit(solution)/shard_map/psum | solution.py:237
  312.8 3.6 copy-start.63
  509.9 4.7 copy-start.24
  514.5 3.3 copy-start.42
  514.5 4.1 copy-start.65
  514.5 4.1 copy-start.64
  514.6 4.1 copy-start.67
  514.6 4.1 copy-start.68
  514.6 87.5 %copy-start.53 = (f32[512]{0:T(512)S(1)}, f32[512]{0:T(512)}, u32[]{:S(2)}) copy-start(f32[512]{0:T(512)} %copy-done.52) | copy-start | bytes 6148
  824.3 4.1 copy-start.41
  (32 other events, 50.7 us)
Sparse Core Ops, SparseCore 0:
  55.8 12.4 all-gather.2
  70.9 10.8 reduce-scatter.6
  96.6 13.5 reduce-scatter.4
  118.2 10.9 all-gather.4
  138.5 9.4 reduce-scatter.10
  154.5 12.0 reduce-scatter.8
  269.2 43.5 all-reduce.10
  321.4 188.4 all-reduce.12
  517.5 298.8 all-reduce.8
